TPU v7x, 32 devices: a whole 2x2x4 slice. The times are simulated.
32 devices in a mesh: row: 8 (over y, x, core), col: 4 (over z).
Axes of the slice: x: 2, y: 2, z: 4, core: 2. Of those that a mesh axis runs over, the one named last changes fastest.
Arguments:
- phase: float32 [4096, 2048], P('row', 'col'), may hold values from -1 to 1
- tile_mask: int32 [16, 8], P('row', 'col'), may hold values 0 or 1
Outputs:
- updated: float32 [4096, 2048], P('row', 'col')
- section: float32 [4096, 2048], P('row', 'col')
All inputs are finite; a program needn't handle non-finite values. No bound on the sum of `tile_mask` on one device may be relied on, other than what follows from the above.
Results may differ from a plain program's by a relative error of at most 0.0003.
Values sent between devices are 32-bit elements; how exact they have to be, the bound alone decides.
A program may use at most 64 MiB of HBM per device.

v0:
```python
import jax
import jax.numpy as jnp
from jax import lax
from jax.sharding import PartitionSpec as P

TILE = 256
KRYLOV = 3


diffusion = 2.0
remainder_weight = 32.0


def extended(cells, sides, width):
    for axis, dim in sides:
        count = lax.axis_size(axis)
        ends = count - 1
        head = lax.slice_in_dim(cells, 0, width, axis=dim)
        tail = lax.slice_in_dim(cells, cells.shape[dim] - width, cells.shape[dim], axis=dim)
        cells = jnp.concatenate(
            [
                lax.ppermute(tail, axis, [(i, (i + 1) % count) for i in range(ends)]),
                cells,
                lax.ppermute(head, axis, [((i + 1) % count, i) for i in range(ends)]),
            ],
            axis=dim,
        )
    return cells


def stencil(padded, field, coef):
    beside = (
        padded[2:, 1:-1] + padded[:-2, 1:-1] + padded[1:-1, 2:] + padded[1:-1, :-2] - 4.0 * field
    )
    return diffusion * beside + coef * field


def operate(field, coef, active):
    padded = extended(field, (("row", 0), ("col", 1)), 1)
    return active * stencil(padded, field, coef)


def exponential(matrix):
    size = matrix.shape[0]
    eye = jnp.eye(size, dtype=jnp.float32)
    scaled = matrix * (1.0 / 1024.0)
    term = eye
    total = eye
    for degree in range(1, 11):
        term = jnp.dot(term, scaled, precision=lax.Precision.HIGHEST) / float(degree)
        total = total + term
    for squaring in range(10):
        total = jnp.dot(total, total, precision=lax.Precision.HIGHEST)
    return total


def phi_column(hess, scale, order):
    width = hess.shape[0]
    size = width + order
    augmented = jnp.zeros((size, size), jnp.float32)
    augmented = augmented.at[:width, :width].set(scale * hess)
    augmented = augmented.at[0, width].set(1.0)
    for offset in range(order - 1):
        augmented = augmented.at[width + offset, width + offset + 1].set(1.0)
    return exponential(augmented)[:width, size - 1]


def arnoldi(start, coef, active):
    buffer = jnp.zeros((KRYLOV,) + start.shape, jnp.float32)
    hess = jnp.zeros((KRYLOV, KRYLOV), jnp.float32)
    current = start
    beta = jnp.float32(1.0)
    for column in range(KRYLOV):
        image = operate(current, coef, active)
        earlier = buffer[: max(column, 1)]
        local_prods = jnp.einsum("krc,rc->k", earlier, image, precision=lax.Precision.HIGHEST)
        square, cross, prods = lax.psum(
            (jnp.sum(current * current), jnp.sum(current * image), local_prods), ("row", "col")
        )
        length = jnp.sqrt(square)
        if column == 0:
            beta = length
        else:
            hess = hess.at[column, column - 1].set(length)
        buffer = buffer.at[column].set(current / length)
        coeffs = jnp.concatenate([prods[:column] / length, jnp.reshape(cross / square, (1,))])
        hess = hess.at[: column + 1, column].set(coeffs)
        if column + 1 < KRYLOV:
            current = image / length - jnp.einsum(
                "k,krc->rc", coeffs, buffer[: column + 1], precision=lax.Precision.HIGHEST
            )
    return (beta, buffer, hess)


def combine(beta, buffer, weights):
    return beta * jnp.einsum("k,krc->rc", weights, buffer, precision=lax.Precision.HIGHEST)


def body(phase, tile_mask):
    tile_rows = tile_mask.shape[0]
    tile_cols = tile_mask.shape[1]
    masks = tile_mask.astype(jnp.float32)
    active = jnp.broadcast_to(masks[:, None, :, None], (tile_rows, TILE, tile_cols, TILE)).reshape(
        tile_rows * TILE, tile_cols * TILE
    )
    force = operate(phase, 1.0 - phase * phase, active)
    slope = 1.0 - 3.0 * phase * phase
    beta_one, basis_one, hess_one = arnoldi(force, slope, active)
    shift = 0.5 * combine(beta_one, basis_one, phi_column(hess_one, 0.5, 1))
    section = phase + shift
    remainder = -active * shift * shift * (shift + 3.0 * phase)
    beta_two, basis_two, hess_two = arnoldi(remainder, slope, active)
    first = combine(beta_one, basis_one, phi_column(hess_one, 1.0, 1))
    third = combine(beta_two, basis_two, phi_column(hess_two, 1.0, 3))
    updated = phase + first + remainder_weight * third
    return (updated, section)


def solution(mesh):
    in_specs = (P("row", "col"), P("row", "col"))
    out_specs = (P("row", "col"), P("row", "col"))
    return jax.shard_map(body, mesh=mesh, in_specs=in_specs, out_specs=out_specs, check_vma=False)
```

profile of v0, /device:TPU:0, one launch (start us, length us, event | category | flops | bytes accessed | tf_op | source)
XLA Modules:
  0.0 509.8 jit_solution(16596849083843773259)
XLA Ops:
  2.8 3.0 collective-permute-start.1
  9.1 5.6 %collective-permute-start.3 = (f32[514,1]{1,0:T(8,128)S(1)}, f32[514,1]{1,0:T(8,128)S(1)}, u32[]{:S(2)}, u32[]{:S(2)}) collective-permute-start(f32[514,1]{1,0:T(8,128)S(1)} %get-tuple-element.341), channel_id=1, source_target_pairs={{0,1},{1,2},{2,3},{4,5},{5,6},{6,7},{8,9},{9,10},{10,11},{12,13},{... | collective-permute-start | bytes 6176 | tf_op jit(solution)/shard_map/ppermute | solution.py:22
  15.8 3.7 collective-permute-done.2
  19.5 1.7 collective-permute-done.3
  23.4 3.0 collective-permute-start.5
  28.6 5.0 collective-permute-start.7
  33.7 3.7 collective-permute-done.6
  37.4 1.7 collective-permute-done.7
  39.1 2.5 multiply_reduce_fusion.15
  41.6 43.1 %all-reduce.12 = (f32[]{:T(128)}, f32[]{:T(128)}) all-reduce(f32[]{:T(128)} %get-tuple-element.301, f32[]{:T(128)} %get-tuple-element.300), channel_id=1, replica_groups=mesh['row'=8,'col'=4] {'row','col'}, use_global_device_ids=true, to_apply=%region_3.0 | all-reduce | flops 2 | bytes 16 | tf_op jit(solution)/shard_map/psum | solution.py:77
  86.6 1.8 fusion.108
  88.5 1.4 collective-permute-start.8
  89.9 3.0 collective-permute-start.9
  95.2 4.6 collective-permute-start.11
  99.8 2.1 scatter.85
  101.9 2.3 collective-permute-done.10
  104.2 1.7 collective-permute-done.11
  105.9 1.5 multiply_reduce_fusion.3
  109.5 43.1 %all-reduce.11 = (f32[]{:T(128)}, f32[]{:T(128)}, f32[1]{0:T(128)}) all-reduce(f32[]{:T(128)} %get-tuple-element.299, f32[]{:T(128)} %get-tuple-element.298, f32[1]{0:T(128)} %bitcast.10), channel_id=1, replica_groups=mesh['row'=8,'col'=4] {'row','col'}, use_global_device_ids=true, to_apply=%region_5.0 | all-reduce | flops 3 | bytes 24 | tf_op jit(solution)/shard_map/psum | solution.py:77
  154.4 3.1 slice.742
  159.3 11.2 %fusion.8 = f32[1,512,512]{2,0,1:T(1,128)S(1)} fusion(f32[2,512,512]{2,1,0:T(8,128)} %slice.742, f32[1]{0:T(128)} %bitcast.12, f32[1]{0:T(128)S(6)} %div.206), kind=kOutput, calls=%fused_computation.10 | convolution fusion | flops 6291458 | bytes 3145736 | tf_op jit(solution)/shard_map/k,krc->rc/dot_general | solution.py:89
  170.5 1.5 bitcast_subtract_fusion.1
  173.3 3.0 collective-permute-start.13
  180.5 5.2 %collective-permute-start.15 = (f32[514,1]{1,0:T(8,128)}, f32[514,1]{1,0:T(8,128)}, u32[]{:S(2)}, u32[]{:S(2)}) collective-permute-start(f32[514,1]{1,0:T(8,128)} %get-tuple-element.335), channel_id=1, source_target_pairs={{0,1},{1,2},{2,3},{4,5},{5,6},{6,7},{8,9},{9,10},{10,11},{12,13},{... | collective-permute-start | bytes 6176 | tf_op jit(solution)/shard_map/ppermute | solution.py:22
  185.9 1.4 scatter.84
  187.3 2.3 collective-permute-done.14
  189.7 1.8 collective-permute-done.15
  191.5 2.4 multiply_reduce_fusion.10
  194.5 41.5 %all-reduce.10 = (f32[]{:T(128)}, f32[]{:T(128)}, f32[2]{0:T(128)S(1)}) all-reduce(f32[]{:T(128)} %get-tuple-element.297, f32[]{:T(128)} %get-tuple-element.296, f32[2]{0:T(128)S(1)} %multiply_reduce_fusion.1), channel_id=1, replica_groups=mesh['row'=8,'col'=4] {'row','col'}, use_global_device_ids=true, to_apply=%region_10.0 | all-reduce | flops 4 | bytes 32 | tf_op jit(solution)/shard_map/psum | solution.py:77
  239.4 2.4 fusion.125
  241.8 1.9 scatter.94
  245.9 2.1 scatter.99
  250.9 12.1 %fusion = f32[1,512,512]{2,0,1:T(1,128)S(1)} fusion(f32[3,1,1]{0,1,2:T(1,128)S(1)} %convolution_bitcast_fusion.1, f32[3,512,512]{2,1,0:T(8,128)} %bitcast_dynamic-update-slice_fusion.2), kind=kOutput, calls=%fused_computation | convolution fusion | flops 9437184 | bytes 4194316 | tf_op jit(solution)/shard_map/k,krc->rc/dot_general | solution.py:96
  262.9 1.4 fusion.68
  265.6 3.0 collective-permute-start.17
  270.9 4.6 collective-permute-start.19
  275.6 4.3 collective-permute-done.18
  279.9 1.7 collective-permute-done.19
  281.7 2.5 multiply_reduce_fusion.9
  284.2 42.4 %all-reduce.9 = (f32[]{:T(128)}, f32[]{:T(128)}) all-reduce(f32[]{:T(128)} %get-tuple-element.295, f32[]{:T(128)} %get-tuple-element.294), channel_id=1, replica_groups=mesh['row'=8,'col'=4] {'row','col'}, use_global_device_ids=true, to_apply=%region_18.0 | all-reduce | flops 2 | bytes 16 | tf_op jit(solution)/shard_map/psum | solution.py:77
  328.6 1.8 fusion.109
  330.4 1.4 collective-permute-start.20
  331.9 3.0 collective-permute-start.21
  337.2 4.6 collective-permute-start.23
  342.0 2.1 scatter.105
  344.1 2.1 collective-permute-done.22
  346.2 1.7 collective-permute-done.23
  347.9 1.6 multiply_reduce_fusion.2
  351.6 42.1 %all-reduce.8 = (f32[]{:T(128)}, f32[]{:T(128)}, f32[1]{0:T(128)}) all-reduce(f32[]{:T(128)} %get-tuple-element.293, f32[]{:T(128)} %get-tuple-element.292, f32[1]{0:T(128)} %bitcast.35), channel_id=1, replica_groups=mesh['row'=8,'col'=4] {'row','col'}, use_global_device_ids=true, to_apply=%region_20.0 | all-reduce | flops 3 | bytes 24 | tf_op jit(solution)/shard_map/psum | solution.py:77
  395.5 3.1 slice.749
  400.6 11.3 %fusion.6 = f32[1,512,512]{2,0,1:T(1,128)S(1)} fusion(f32[2,512,512]{2,1,0:T(8,128)} %slice.749, f32[1]{0:T(128)} %bitcast.37, f32[1]{0:T(128)S(6)} %div.238), kind=kOutput, calls=%fused_computation.8 | convolution fusion | flops 6291458 | bytes 3145736 | tf_op jit(solution)/shard_map/k,krc->rc/dot_general | solution.py:89
  411.9 1.5 bitcast_subtract_fusion
  414.7 3.0 collective-permute-start.25
  417.7 9.8 %fusion.2 = f32[1,512,512]{2,0,1:T(1,128)} fusion(f32[3,1,1]{0,1,2:T(1,128)S(1)} %convolution_bitcast_fusion.2, f32[3,512,512]{2,1,0:T(8,128)S(1)} %copy-done.2), kind=kOutput, calls=%fused_computation.2 | convolution fusion | flops 9437184 | bytes 4194316 | tf_op jit(solution)/shard_map/k,krc->rc/dot_general | solution.py:96
  429.8 5.3 %collective-permute-start.27 = (f32[514,1]{1,0:T(8,128)}, f32[514,1]{1,0:T(8,128)}, u32[]{:S(2)}, u32[]{:S(2)}) collective-permute-start(f32[514,1]{1,0:T(8,128)} %get-tuple-element.329), channel_id=1, source_target_pairs={{0,1},{1,2},{2,3},{4,5},{5,6},{6,7},{8,9},{9,10},{10,11},{12,13},{... | collective-permute-start | bytes 6176 | tf_op jit(solution)/shard_map/ppermute | solution.py:22
  435.5 1.4 scatter.104
  436.8 2.1 collective-permute-done.26
  438.9 1.8 collective-permute-done.27
  440.8 2.5 multiply_reduce_fusion.4
  443.8 41.4 %all-reduce.7 = (f32[]{:T(128)}, f32[]{:T(128)}, f32[2]{0:T(128)S(1)}) all-reduce(f32[]{:T(128)} %get-tuple-element.291, f32[]{:T(128)} %get-tuple-element.290, f32[2]{0:T(128)S(1)} %multiply_reduce_fusion), channel_id=1, replica_groups=mesh['row'=8,'col'=4] {'row','col'}, use_global_device_ids=true, to_apply=%region_25.0 | all-reduce | flops 4 | bytes 32 | tf_op jit(solution)/shard_map/psum | solution.py:77
  488.6 2.4 fusion.126
  490.9 1.8 scatter.114
  495.9 12.1 %fusion.4 = f32[1,512,512]{2,0,1:T(1,128)S(1)} fusion(f32[3,1,1]{0,1,2:T(1,128)S(1)} %convolution_bitcast_fusion, f32[3,512,512]{2,1,0:T(8,128)} %bitcast_dynamic-update-slice_fusion), kind=kOutput, calls=%fused_computation.4 | convolution fusion | flops 9437184 | bytes 4194316 | tf_op jit(solution)/shard_map/k,krc->rc/dot_general | solution.py:96
  508.0 1.3 fusion.65
  (160 shorter events, 47.0 us)
Async XLA Ops:
  0.6 20.6 %copy-start = (f32[512,512]{1,0:T(8,128)S(1)}, f32[512,512]{1,0:T(8,128)}, u32[]{:S(2)}) copy-start(f32[512,512]{1,0:T(8,128)} %param.50) | copy-start | bytes 3145732
  1.5 4.3 collective-permute-start
  2.8 3.8 collective-permute-start.1
  7.8 11.7 %collective-permute-start.2 = (f32[514,1]{1,0:T(8,128)S(1)}, f32[514,1]{1,0:T(8,128)S(1)}, u32[]{:S(2)}, u32[]{:S(2)}) collective-permute-start(f32[514,1]{1,0:T(8,128)S(1)} %get-tuple-element.340), channel_id=1, source_target_pairs={{1,0},{2,1},{3,2},{5,4},{6,5},{7,6},{9,8},{10,9},{11,10},{13,12},{... | collective-permute-start | bytes 6176 | tf_op jit(solution)/shard_map/ppermute | solution.py:24
  9.1 12.1 %collective-permute-start.3 = (f32[514,1]{1,0:T(8,128)S(1)}, f32[514,1]{1,0:T(8,128)S(1)}, u32[]{:S(2)}, u32[]{:S(2)}) collective-permute-start(f32[514,1]{1,0:T(8,128)S(1)} %get-tuple-element.341), channel_id=1, source_target_pairs={{0,1},{1,2},{2,3},{4,5},{5,6},{6,7},{8,9},{9,10},{10,11},{12,13},{... | collective-permute-start | bytes 6176 | tf_op jit(solution)/shard_map/ppermute | solution.py:22
  22.0 19.6 %copy-start.6 = (f32[512,512]{1,0:T(8,128)}, f32[512,512]{1,0:T(8,128)S(1)}, u32[]{:S(2)}) copy-start(f32[512,512]{1,0:T(8,128)S(1)} %fusion.61) | copy-start | bytes 3145732
  22.1 4.3 collective-permute-start.4
  23.4 3.8 collective-permute-start.5
  27.3 10.0 %collective-permute-start.6 = (f32[514,1]{1,0:T(8,128)S(1)}, f32[514,1]{1,0:T(8,128)S(1)}, u32[]{:S(2)}, u32[]{:S(2)}) collective-permute-start(f32[514,1]{1,0:T(8,128)S(1)} %get-tuple-element.338), channel_id=1, source_target_pairs={{1,0},{2,1},{3,2},{5,4},{6,5},{7,6},{9,8},{10,9},{11,10},{13,12},{... | collective-permute-start | bytes 6176 | tf_op jit(solution)/shard_map/ppermute | solution.py:24
  28.6 10.4 %collective-permute-start.7 = (f32[514,1]{1,0:T(8,128)S(1)}, f32[514,1]{1,0:T(8,128)S(1)}, u32[]{:S(2)}, u32[]{:S(2)}) collective-permute-start(f32[514,1]{1,0:T(8,128)S(1)} %get-tuple-element.339), channel_id=1, source_target_pairs={{0,1},{1,2},{2,3},{4,5},{5,6},{6,7},{8,9},{9,10},{10,11},{12,13},{... | collective-permute-start | bytes 6176 | tf_op jit(solution)/shard_map/ppermute | solution.py:22
  88.4 17.5 %copy-start.7 = (f32[512,512]{1,0:T(8,128)S(1)}, f32[512,512]{1,0:T(8,128)}, u32[]{:S(2)}) copy-start(f32[512,512]{1,0:T(8,128)} %copy-done.6) | copy-start | bytes 3145732
  88.5 5.1 collective-permute-start.8
  89.9 3.8 collective-permute-start.9
  93.9 10.3 %collective-permute-start.10 = (f32[514,1]{1,0:T(8,128)S(1)}, f32[514,1]{1,0:T(8,128)S(1)}, u32[]{:S(2)}, u32[]{:S(2)}) collective-permute-start(f32[514,1]{1,0:T(8,128)S(1)} %get-tuple-element.336), channel_id=1, source_target_pairs={{1,0},{2,1},{3,2},{5,4},{6,5},{7,6},{9,8},{10,9},{11,10},{13,12},{... | collective-permute-start | bytes 6176 | tf_op jit(solution)/shard_map/ppermute | solution.py:24
  95.2 10.8 %collective-permute-start.11 = (f32[514,1]{1,0:T(8,128)S(1)}, f32[514,1]{1,0:T(8,128)S(1)}, u32[]{:S(2)}, u32[]{:S(2)}) collective-permute-start(f32[514,1]{1,0:T(8,128)S(1)} %get-tuple-element.337), channel_id=1, source_target_pairs={{0,1},{1,2},{2,3},{4,5},{5,6},{6,7},{8,9},{9,10},{10,11},{12,13},{... | collective-permute-start | bytes 6176 | tf_op jit(solution)/shard_map/ppermute | solution.py:22
  107.5 1.0 copy-start.8
  172.0 6.3 %collective-permute-start.12 = (f32[1,512]{1,0:T(1,128)S(1)}, f32[1,512]{1,0:T(1,128)S(1)}, u32[]{:S(2)}, u32[]{:S(2)}) collective-permute-start(f32[1,512]{1,0:T(1,128)S(1)} %get-tuple-element.351), channel_id=1, source_target_pairs={{4,0},{8,4},{12,8},{16,12},{20,16},{24,20},{28,24},{5,1},{9,5},{13... | collective-permute-start | bytes 6152 | tf_op jit(solution)/shard_map/ppermute | solution.py:24
  173.3 5.0 collective-permute-start.13
  179.2 10.4 %collective-permute-start.14 = (f32[514,1]{1,0:T(8,128)}, f32[514,1]{1,0:T(8,128)S(1)}, u32[]{:S(2)}, u32[]{:S(2)}) collective-permute-start(f32[514,1]{1,0:T(8,128)} %get-tuple-element.334), channel_id=1, source_target_pairs={{1,0},{2,1},{3,2},{5,4},{6,5},{7,6},{9,8},{10,9},{11,10},{13,12},{... | collective-permute-start | bytes 6176 | tf_op jit(solution)/shard_map/ppermute | solution.py:24
  180.5 11.0 %collective-permute-start.15 = (f32[514,1]{1,0:T(8,128)}, f32[514,1]{1,0:T(8,128)}, u32[]{:S(2)}, u32[]{:S(2)}) collective-permute-start(f32[514,1]{1,0:T(8,128)} %get-tuple-element.335), channel_id=1, source_target_pairs={{0,1},{1,2},{2,3},{4,5},{5,6},{6,7},{8,9},{9,10},{10,11},{12,13},{... | collective-permute-start | bytes 6176 | tf_op jit(solution)/shard_map/ppermute | solution.py:22
  187.3 6.6 %copy-start.1 = (f32[3,512,512]{2,1,0:T(8,128)S(1)}, f32[3,512,512]{2,1,0:T(8,128)}, u32[]{:S(2)}) copy-start(f32[3,512,512]{2,1,0:T(8,128)} %bitcast_dynamic-update-slice_fusion.3) | copy-start | bytes 9437188
  264.3 19.9 %copy-start.4 = (f32[512,512]{1,0:T(8,128)}, f32[512,512]{1,0:T(8,128)S(1)}, u32[]{:S(2)}) copy-start(f32[512,512]{1,0:T(8,128)S(1)} %get-tuple-element.327) | copy-start | bytes 3145732
  264.3 4.5 collective-permute-start.16
  265.6 3.8 collective-permute-start.17
  269.6 10.3 %collective-permute-start.18 = (f32[514,1]{1,0:T(8,128)S(1)}, f32[514,1]{1,0:T(8,128)S(1)}, u32[]{:S(2)}, u32[]{:S(2)}) collective-permute-start(f32[514,1]{1,0:T(8,128)S(1)} %get-tuple-element.332), channel_id=1, source_target_pairs={{1,0},{2,1},{3,2},{5,4},{6,5},{7,6},{9,8},{10,9},{11,10},{13,12},{... | collective-permute-start | bytes 6176 | tf_op jit(solution)/shard_map/ppermute | solution.py:24
  270.9 10.8 %collective-permute-start.19 = (f32[514,1]{1,0:T(8,128)S(1)}, f32[514,1]{1,0:T(8,128)S(1)}, u32[]{:S(2)}, u32[]{:S(2)}) collective-permute-start(f32[514,1]{1,0:T(8,128)S(1)} %get-tuple-element.333), channel_id=1, source_target_pairs={{0,1},{1,2},{2,3},{4,5},{5,6},{6,7},{8,9},{9,10},{10,11},{12,13},{... | collective-permute-start | bytes 6176 | tf_op jit(solution)/shard_map/ppermute | solution.py:22
  330.4 17.5 %copy-start.5 = (f32[512,512]{1,0:T(8,128)S(1)}, f32[512,512]{1,0:T(8,128)}, u32[]{:S(2)}) copy-start(f32[512,512]{1,0:T(8,128)} %copy-done.4) | copy-start | bytes 3145732
  330.4 4.6 collective-permute-start.20
  331.9 3.8 collective-permute-start.21
  335.9 10.3 %collective-permute-start.22 = (f32[514,1]{1,0:T(8,128)S(1)}, f32[514,1]{1,0:T(8,128)S(1)}, u32[]{:S(2)}, u32[]{:S(2)}) collective-permute-start(f32[514,1]{1,0:T(8,128)S(1)} %get-tuple-element.330), channel_id=1, source_target_pairs={{1,0},{2,1},{3,2},{5,4},{6,5},{7,6},{9,8},{10,9},{11,10},{13,12},{... | collective-permute-start | bytes 6176 | tf_op jit(solution)/shard_map/ppermute | solution.py:24
  337.2 10.8 %collective-permute-start.23 = (f32[514,1]{1,0:T(8,128)S(1)}, f32[514,1]{1,0:T(8,128)S(1)}, u32[]{:S(2)}, u32[]{:S(2)}) collective-permute-start(f32[514,1]{1,0:T(8,128)S(1)} %get-tuple-element.331), channel_id=1, source_target_pairs={{0,1},{1,2},{2,3},{4,5},{5,6},{6,7},{8,9},{9,10},{10,11},{12,13},{... | collective-permute-start | bytes 6176 | tf_op jit(solution)/shard_map/ppermute | solution.py:22
  349.5 1.0 copy-start.9
  400.5 17.2 %copy-start.2 = (f32[3,512,512]{2,1,0:T(8,128)S(1)}, f32[3,512,512]{2,1,0:T(8,128)}, u32[]{:S(2)}) copy-start(f32[3,512,512]{2,1,0:T(8,128)} %bitcast_dynamic-update-slice_fusion.2) | copy-start | bytes 9437188
  413.4 14.2 %collective-permute-start.24 = (f32[1,512]{1,0:T(1,128)S(1)}, f32[1,512]{1,0:T(1,128)S(1)}, u32[]{:S(2)}, u32[]{:S(2)}) collective-permute-start(f32[1,512]{1,0:T(1,128)S(1)} %get-tuple-element.343), channel_id=1, source_target_pairs={{4,0},{8,4},{12,8},{16,12},{20,16},{24,20},{28,24},{5,1},{9,5},{13... | collective-permute-start | bytes 6152 | tf_op jit(solution)/shard_map/ppermute | solution.py:24
  414.7 12.9 %collective-permute-start.25 = (f32[1,512]{1,0:T(1,128)S(1)}, f32[1,512]{1,0:T(1,128)S(1)}, u32[]{:S(2)}, u32[]{:S(2)}) collective-permute-start(f32[1,512]{1,0:T(1,128)S(1)} %get-tuple-element.342), channel_id=1, source_target_pairs={{0,4},{4,8},{8,12},{12,16},{16,20},{20,24},{24,28},{1,5},{5,9},{9,... | collective-permute-start | bytes 6152 | tf_op jit(solution)/shard_map/ppermute | solution.py:22
  428.5 10.4 %collective-permute-start.26 = (f32[514,1]{1,0:T(8,128)}, f32[514,1]{1,0:T(8,128)S(1)}, u32[]{:S(2)}, u32[]{:S(2)}) collective-permute-start(f32[514,1]{1,0:T(8,128)} %get-tuple-element.328), channel_id=1, source_target_pairs={{1,0},{2,1},{3,2},{5,4},{6,5},{7,6},{9,8},{10,9},{11,10},{13,12},{... | collective-permute-start | bytes 6176 | tf_op jit(solution)/shard_map/ppermute | solution.py:24
  429.8 11.0 %collective-permute-start.27 = (f32[514,1]{1,0:T(8,128)}, f32[514,1]{1,0:T(8,128)}, u32[]{:S(2)}, u32[]{:S(2)}) collective-permute-start(f32[514,1]{1,0:T(8,128)} %get-tuple-element.329), channel_id=1, source_target_pairs={{0,1},{1,2},{2,3},{4,5},{5,6},{6,7},{8,9},{9,10},{10,11},{12,13},{... | collective-permute-start | bytes 6176 | tf_op jit(solution)/shard_map/ppermute | solution.py:22
  436.8 6.4 %copy-start.3 = (f32[3,512,512]{2,1,0:T(8,128)S(1)}, f32[3,512,512]{2,1,0:T(8,128)}, u32[]{:S(2)}) copy-start(f32[3,512,512]{2,1,0:T(8,128)} %bitcast_dynamic-update-slice_fusion.1) | copy-start | bytes 9437188
  487.0 21.0 %copy-start.10 = (f32[1,512,512]{2,0,1:T(1,128)S(1)}, f32[1,512,512]{2,0,1:T(1,128)}, u32[]{:S(2)}) copy-start(f32[1,512,512]{2,0,1:T(1,128)} %fusion.2) | copy-start | bytes 3145732
where the time goes:
time: 517 us; the launch traced here: 510 us
  blocking collectives  254 us (49%)
  starting transfers between devices  74.3 us (14%)
  matrix products  65.1 us (13%)
  other arithmetic  41.4 us (8%)
  waiting for transfers between devices  36.1 us (7%)
  local copies, waits for them, and re-layouts  24.3 us (5%)
  between operations  14.9 us (3%)
    psum x6, blocking collectives, arnoldi(): lax.psum((jnp.sum(current * current), jnp.sum(current * image), local_pro...  254 us
    ppermute x14, starting transfers between devices, extended(): lax.ppermute(tail, axis, [(i, (i + 1) % count) for i in range(ends)])  56 us
    dot_general x3, matrix products, combine(): jnp.einsum('k,krc->rc', weights, buffer, precision=lax.Precision.HIGHEST)  33.9 us
    dot_general x2, matrix products, arnoldi(): jnp.einsum('k,krc->rc', coeffs, buffer[:column + 1], precision=lax.Precis...  22.5 us
    ppermute x14, waiting for transfers between devices, extended(): lax.ppermute(head, axis, [((i + 1) % count, i) for i in range(ends)])  20.6 us
    ppermute x14, starting transfers between devices, extended(): lax.ppermute(head, axis, [((i + 1) % count, i) for i in range(ends)])  18.3 us
    ppermute x14, waiting for transfers between devices, extended(): lax.ppermute(tail, axis, [(i, (i + 1) % count) for i in range(ends)])  15.5 us
  transfers between devices with their start and end apart: 28, of which 19 were waited for; matrix products, arithmetic and copies ran while one was open for 4% of the time, Pallas kernels for 0%

commit v1 on v0

v1 whole, which is shorter than its diff:
```python
import functools

import jax
import jax.numpy as jnp
from jax import lax
from jax.experimental import pallas as pl
from jax.experimental.pallas import tpu as pltpu
from jax.sharding import PartitionSpec as P

TILE = 256
HALO = 8
LANES = 128
CHUNK = 16
MOMENTS = 6
MESH = pl.DeviceIdType.MESH

diffusion = 2.0
remainder_weight = 32.0
offset = -4.0 * diffusion

STEPS = ((-1, 0), (1, 0), (0, -1), (0, 1), (-1, -1), (-1, 1), (1, -1), (1, 1))
OPPOSITE = (1, 0, 3, 2, 7, 6, 5, 4)


def phi_weights(diag, lower_sq, scale, order):
    s = scale * (1.0 / 1024.0)
    zero = jnp.zeros_like(s)
    one = jnp.ones_like(s)
    hess = [
        [diag[0] * s, lower_sq[0] * s, None],
        [s, diag[1] * s, lower_sq[1] * s],
        [None, s, diag[2] * s],
    ]
    eps = 1.0 / 1024.0
    term = [[one if i == j else zero for j in range(3)] for i in range(3)]
    total = [row[:] for row in term]
    side_term = [[zero] * order for _ in range(3)]
    side = [[zero] * order for _ in range(3)]
    tail = [1.0]
    for k in range(1, order):
        tail.append(tail[-1] * eps / k)
    for degree in range(1, 11):
        inv = 1.0 / degree
        new_term, new_side = [], []
        for i in range(3):
            row = []
            for j in range(3):
                acc = None
                for k in range(3):
                    if hess[k][j] is not None:
                        part = term[i][k] * hess[k][j]
                        acc = part if acc is None else acc + part
                row.append(acc * inv)
            new_term.append(row)
            new_side.append(
                [(term[i][0] if c == 0 else side_term[i][c - 1]) * (eps * inv) for c in range(order)]
            )
        term, side_term = new_term, new_side
        total = [[total[i][j] + term[i][j] for j in range(3)] for i in range(3)]
        side = [[side[i][c] + side_term[i][c] for c in range(order)] for i in range(3)]
    for _ in range(10):
        new_side = []
        for i in range(3):
            row = []
            for c in range(order):
                acc = side[i][c]
                for k in range(c):
                    acc = acc + side[i][k] * tail[c - k]
                for k in range(3):
                    acc = acc + total[i][k] * side[k][c]
                row.append(acc)
            new_side.append(row)
        total = [
            [
                total[i][0] * total[0][j] + total[i][1] * total[1][j] + total[i][2] * total[2][j]
                for j in range(3)
            ]
            for i in range(3)
        ]
        side = new_side
        tail = [sum(tail[k] * tail[c - k] for k in range(c + 1)) for c in range(order)]
    return [side[i][order - 1] for i in range(3)]


def lanczos(m):
    tiny = 1e-7
    a0 = m[1] / m[0]
    n1 = jnp.maximum(m[2] - a0 * m[1], tiny * m[2])
    h1 = n1 / m[0]
    a1 = (m[3] - 2.0 * a0 * m[2] + a0 * a0 * m[1]) / n1
    c1 = -(a0 + a1)
    c0 = a0 * a1 - h1
    n2 = jnp.maximum(m[4] + c1 * m[3] + c0 * m[2], tiny * m[4])
    h2 = n2 / n1
    a2 = (
        m[5] + 2.0 * c1 * m[4] + (c1 * c1 + 2.0 * c0) * m[3] + 2.0 * c0 * c1 * m[2] + c0 * c0 * m[1]
    ) / n2
    diag = [a0 + offset, a1 + offset, a2 + offset]
    return diag, [h1, h2], (a0, c1, c0)


def to_powers(y, coefs):
    a0, c1, c0 = coefs
    return (y[0] - a0 * y[1] + c0 * y[2], y[1] + c1 * y[2], y[2])


def kernel(
    n_row, n_col, phase_hbm, mask_ref, upd_hbm, sec_hbm,
    ph, a2, q, u0, u1, u2, w0, w1, w2, upd, sec,
    out_strip, in_side, in_corner, row_buf, gather,
    local_sem, side_send, side_recv, red_send, red_recv,
):
    rows, cols = upd.shape
    width = cols + LANES
    tall = rows + 2 * HALO
    n_dev = n_row * n_col
    my_row = lax.axis_index("row")
    my_col = lax.axis_index("col")
    me = my_row * n_col + my_col

    load = pltpu.make_async_copy(
        phase_hbm, ph.at[pl.ds(HALO, rows), pl.ds(0, cols)], local_sem.at[0]
    )
    load.start()

    barrier = pltpu.get_barrier_semaphore()

    def peer_of(d):
        peer = lax.rem(me + d, n_dev)
        return {"row": peer // n_col, "col": lax.rem(peer, n_col)}

    def greet(d, carry):
        pl.semaphore_signal(barrier, inc=1, device_id=peer_of(d), device_id_type=MESH)
        return carry

    lax.fori_loop(1, n_dev, greet, 0)

    def exists(k):
        dr, dc = STEPS[k]
        ok = None
        for cond in (
            my_row > 0 if dr < 0 else (my_row < n_row - 1 if dr > 0 else None),
            my_col > 0 if dc < 0 else (my_col < n_col - 1 if dc > 0 else None),
        ):
            if cond is not None:
                ok = cond if ok is None else jnp.logical_and(ok, cond)
        return ok

    def landing(k):
        return in_side.at[k] if k < 4 else in_corner.at[k - 4]

    def source(k):
        if k < 4:
            return out_strip.at[k]
        dr, dc = STEPS[k]
        return out_strip.at[0 if dr < 0 else 1, :, pl.ds(0 if dc < 0 else cols - LANES, LANES)]

    for k in range(8):
        @pl.when(jnp.logical_not(exists(k)))
        def _(k=k):
            if k < 4:
                in_side[k] = jnp.zeros((2 * HALO, cols), jnp.float32)
            else:
                in_corner[k - 4] = jnp.zeros((2 * HALO, LANES), jnp.float32)

    tile_rows, tile_cols = rows // TILE, cols // TILE
    value = [
        [mask_ref[i, j].astype(jnp.float32) * diffusion for j in range(tile_cols)]
        for i in range(tile_rows)
    ]
    for j in range(tile_cols):
        cut = pl.ds(j * TILE, TILE)
        out_strip[0, HALO:, cut] = jnp.full((HALO, TILE), value[0][j], jnp.float32)
        out_strip[1, HALO:, cut] = jnp.full((HALO, TILE), value[-1][j], jnp.float32)
        for i in range(tile_rows):
            a2[pl.ds(HALO + i * TILE, TILE), cut] = jnp.full((TILE, TILE), value[i][j], jnp.float32)
    for i in range(tile_rows):
        cut = pl.ds(i * TILE, TILE)
        out_strip[2, HALO:, cut] = jnp.full((HALO, TILE), value[i][0], jnp.float32)
        out_strip[3, HALO:, cut] = jnp.full((HALO, TILE), value[i][-1], jnp.float32)

    load.wait()
    out_strip[0, :HALO, :] = ph[pl.ds(HALO, HALO), pl.ds(0, cols)]
    out_strip[1, :HALO, :] = ph[pl.ds(rows, HALO), pl.ds(0, cols)]
    out_strip[2, :HALO, :] = ph[pl.ds(HALO, rows), pl.ds(0, LANES)].T[:HALO]
    out_strip[3, :HALO, :] = ph[pl.ds(HALO, rows), pl.ds(cols - LANES, LANES)].T[LANES - HALO:]

    pl.semaphore_wait(barrier, n_dev - 1)

    def side_copy(k):
        dr, dc = STEPS[k]
        return pltpu.make_async_remote_copy(
            src_ref=source(k),
            dst_ref=landing(OPPOSITE[k]),
            send_sem=side_send.at[k],
            recv_sem=side_recv.at[OPPOSITE[k]],
            device_id={"row": my_row + dr, "col": my_col + dc},
            device_id_type=MESH,
        )

    def side_arrival(k):
        dr, dc = STEPS[k]
        return pltpu.make_async_remote_copy(
            src_ref=landing(k),
            dst_ref=landing(k),
            send_sem=side_send.at[k],
            recv_sem=side_recv.at[k],
            device_id={"row": my_row + dr, "col": my_col + dc},
            device_id_type=MESH,
        )

    for k in range(8):
        @pl.when(exists(k))
        def _(k=k):
            side_copy(k).start()
    for k in range(8):
        @pl.when(exists(k))
        def _(k=k):
            side_arrival(k).wait_recv()

    lane = lax.broadcasted_iota(jnp.int32, (HALO, LANES), 1)
    halo_lanes = pl.ds(cols, LANES)
    gap = jnp.zeros((LANES - 2 * HALO, rows), jnp.float32)
    for part, ref in ((slice(0, HALO), ph), (slice(HALO, 2 * HALO), a2)):
        ref[pl.ds(0, HALO), pl.ds(0, cols)] = in_side[0, part, :]
        ref[pl.ds(HALO + rows, HALO), pl.ds(0, cols)] = in_side[1, part, :]
        ref[pl.ds(HALO, rows), halo_lanes] = jnp.concatenate(
            [in_side[3, part, :], gap, in_side[2, part, :]], axis=0
        ).T
        ref[pl.ds(0, HALO), halo_lanes] = jnp.where(
            lane < LANES // 2, in_corner[1, part, :], in_corner[0, part, :]
        )
        ref[pl.ds(HALO + rows, HALO), halo_lanes] = jnp.where(
            lane < LANES // 2, in_corner[3, part, :], in_corner[2, part, :]
        )

    def around(x, low, count):
        high = x.shape[0]
        centre = x[low:low + count]
        total = (
            pltpu.roll(x, 1, 0)[low:low + count]
            + pltpu.roll(x, high - 1, 0)[low:low + count]
            + pltpu.roll(centre, 1, 1)
            + pltpu.roll(centre, width - 1, 1)
        )
        return centre, total

    def fold(x):
        total = None
        for i in range(0, x.shape[0], 8):
            for j in range(0, cols, LANES):
                piece = x[i:i + 8, j:j + LANES]
                total = piece if total is None else total + piece
        return total

    def sweep(field, finish, n_sums, halo):
        if halo:
            finish(*around(field[pl.ds(0, 2 * HALO), :], 0, HALO), pl.ds(0, HALO))
            finish(
                *around(field[pl.ds(tall - 2 * HALO, 2 * HALO), :], HALO, HALO),
                pl.ds(tall - HALO, HALO),
            )

        def step(i, sums):
            start = pl.multiple_of(i * CHUNK, 8)
            x = field[pl.ds(start, CHUNK + 2 * HALO), :]
            terms = finish(
                *around(x, HALO, CHUNK), pl.ds(pl.multiple_of(start + HALO, 8), CHUNK)
            )
            return tuple(s + fold(t) for s, t in zip(sums, terms))

        zero = jnp.zeros((8, LANES), jnp.float32)
        return lax.fori_loop(0, rows // CHUNK, step, (zero,) * n_sums)

    def force_of(centre, near, at):
        act2 = a2[at, :]
        square = centre * centre
        act = act2 * (1.0 / diffusion)
        q[at, :] = act * (1.0 - 3.0 * square)
        u0[at, :] = act2 * (near - 4.0 * centre) + act * ((1.0 - square) * centre)
        return ()

    sweep(ph, force_of, 0, True)

    def power(dst, with_start):
        def finish(centre, near, at):
            image = a2[at, :] * near + q[at, :] * centre
            if dst is not None:
                dst[at, :] = image
            cross = centre * image
            if dst is None:
                return (cross,)
            if with_start:
                return (centre * centre, cross, image * image)
            return (cross, image * image)

        return finish

    def moments(b0, b1, b2, index):
        sums = sweep(b0, power(b1, True), 3, True)
        sums += sweep(b1, power(b2, False), 2, True)
        sums += sweep(b2, power(None, False), 1, False)
        lanes = lax.broadcasted_iota(jnp.int32, (1, LANES), 1)
        row = jnp.zeros((1, LANES), jnp.float32)
        for k, s in enumerate(sums):
            row = jnp.where(lanes == k, jnp.sum(s, keepdims=True), row)
        row_buf[index] = row
        gather[index, me] = row

        def send(d, carry):
            pltpu.make_async_remote_copy(
                src_ref=row_buf.at[index],
                dst_ref=gather.at[index, me],
                send_sem=red_send.at[index],
                recv_sem=red_recv.at[index],
                device_id=peer_of(d),
                device_id_type=MESH,
            ).start()
            return carry

        lax.fori_loop(1, n_dev, send, 0)
        others = gather.at[index, pl.ds(0, n_dev - 1)]
        done = pltpu.make_async_remote_copy(
            src_ref=others,
            dst_ref=others,
            send_sem=red_send.at[index],
            recv_sem=red_recv.at[index],
            device_id=peer_of(1),
            device_id_type=MESH,
        )
        done.wait_recv()
        done.wait_send()
        total = jnp.sum(gather[index], axis=0)
        total = jnp.broadcast_to(total, (8, LANES))
        spot = lax.broadcasted_iota(jnp.int32, (8, LANES), 1)
        return [
            jnp.broadcast_to(
                jnp.sum(jnp.where(spot == k, total, 0.0), axis=1, keepdims=True), (8, LANES)
            )
            for k in range(MOMENTS)
        ]

    def spread(x, count, wide):
        return jnp.broadcast_to(x, (count, wide))

    diag, lower, coefs = lanczos(moments(u0, u1, u2, 0))
    sub = lax.broadcasted_iota(jnp.int32, (8, LANES), 0)
    scale = jnp.where(sub < 4, 0.5, 1.0).astype(jnp.float32)
    mixed = to_powers(phi_weights(diag, lower, scale, 1), coefs)
    half = [0.5 * m[0:1, 0:1] for m in mixed]
    full = [m[4:5, 0:1] for m in mixed]

    def section_of(at, out_at):
        x0, x1, x2 = u0[at, :], u1[at, :], u2[at, :]
        here = ph[at, :]
        shift = half[0] * x0 + half[1] * x1 + half[2] * x2
        w0[at, :] = (a2[at, :] * (-1.0 / diffusion)) * shift * shift * (shift + 3.0 * here)
        if out_at is not None:
            sec[out_at, :] = (here + shift)[:, :cols]
            upd[out_at, :] = (here + full[0] * x0 + full[1] * x1 + full[2] * x2)[:, :cols]

    section_of(pl.ds(0, HALO), None)
    section_of(pl.ds(tall - HALO, HALO), None)

    def section_step(i, carry):
        start = pl.multiple_of(i * CHUNK, 8)
        section_of(pl.ds(pl.multiple_of(start + HALO, 8), CHUNK), pl.ds(start, CHUNK))
        return carry

    lax.fori_loop(0, rows // CHUNK, section_step, 0)
    put_sec = pltpu.make_async_copy(sec, sec_hbm, local_sem.at[1])
    put_sec.start()

    diag, lower, coefs = lanczos(moments(w0, w1, w2, 1))
    third = [
        remainder_weight * m[0:1, 0:1]
        for m in to_powers(phi_weights(diag, lower, jnp.ones((8, LANES), jnp.float32), 3), coefs)
    ]

    def final_step(i, carry):
        start = pl.multiple_of(i * CHUNK, 8)
        at = pl.ds(pl.multiple_of(start + HALO, 8), CHUNK)
        cut = pl.ds(0, cols)
        out_at = pl.ds(start, CHUNK)
        upd[out_at, :] = upd[out_at, :] + (
            third[0] * w0[at, cut] + third[1] * w1[at, cut] + third[2] * w2[at, cut]
        )
        return carry

    lax.fori_loop(0, rows // CHUNK, final_step, 0)
    put_upd = pltpu.make_async_copy(upd, upd_hbm, local_sem.at[2])
    put_upd.start()
    for k in range(8):
        @pl.when(exists(k))
        def _(k=k):
            side_copy(k).wait_send()
    put_sec.wait()
    put_upd.wait()


def body(n_row, n_col, phase, tile_mask):
    rows, cols = phase.shape
    n_dev = n_row * n_col
    block = pltpu.VMEM((rows + 2 * HALO, cols + LANES), jnp.float32)
    flat = pltpu.VMEM((rows, cols), jnp.float32)
    shape = jax.ShapeDtypeStruct((rows, cols), jnp.float32)
    hbm = pl.BlockSpec(memory_space=pl.ANY)
    return pl.pallas_call(
        functools.partial(kernel, n_row, n_col),
        out_shape=(shape, shape),
        in_specs=[hbm, pl.BlockSpec(memory_space=pltpu.SMEM)],
        out_specs=(hbm, hbm),
        scratch_shapes=[block] * 9 + [flat] * 2 + [
            pltpu.VMEM((4, 2 * HALO, cols), jnp.float32),
            pltpu.VMEM((4, 2 * HALO, cols), jnp.float32),
            pltpu.VMEM((4, 2 * HALO, LANES), jnp.float32),
            pltpu.VMEM((2, 1, LANES), jnp.float32),
            pltpu.VMEM((2, n_dev, 1, LANES), jnp.float32),
            pltpu.SemaphoreType.DMA((3,)),
            pltpu.SemaphoreType.DMA((8,)),
            pltpu.SemaphoreType.DMA((8,)),
            pltpu.SemaphoreType.DMA((2,)),
            pltpu.SemaphoreType.DMA((2,)),
        ],
        compiler_params=pltpu.CompilerParams(collective_id=0, has_side_effects=True),
        name="epirk_section",
    )(phase, tile_mask)


def solution(mesh):
    spec = P("row", "col")
    run = functools.partial(body, mesh.shape["row"], mesh.shape["col"])
    return jax.shard_map(
        run, mesh=mesh, in_specs=(spec, spec), out_specs=(spec, spec), check_vma=False
    )
```

time: 517 us -> 49.9 us (0.10); the launches traced: 510 us -> 49.7 us
  blocking collectives: 254 us -> 0 us
  starting transfers between devices: 74.3 us -> 0 us
  matrix products: 65.1 us -> 0 us
  Pallas kernels: 0 us -> 45.7 us
  other arithmetic: 41.4 us -> 0 us
  waiting for transfers between devices: 36.1 us -> 0 us
  local copies, waits for them, and re-layouts: 24.3 us -> 3.32 us
  between operations: 14.9 us -> 0.65 us
    psum x6 -> x0, blocking collectives: 254 us -> none  [arnoldi(): lax.psum((jnp.sum(current * current), jnp.sum(current * image), local_pro...]
    ppermute x28 -> x0, starting transfers between devices: 74.3 us -> none  [the longest x14 56 us: extended(): lax.ppermute(tail, axis, [(i, (i + 1) % count) for i in range(ends)])]
    dot_general x65 -> x0, matrix products: 65.1 us -> none  [the longest x3 33.9 us: combine(): jnp.einsum('k,krc->rc', weights, buffer, precision=lax.Precision.HIGHEST)]
    pallas_call x0 -> x1, Pallas kernels: none -> 45.7 us  [body(): pl.pallas_call(functools.partial(kernel, n_row, n_col), out_shape=(shape,...]
    ppermute x28 -> x0, waiting for transfers between devices: 36.1 us -> none  [the longest x14 20.6 us: extended(): lax.ppermute(head, axis, [((i + 1) % count, i) for i in range(ends)])]
    scatter x20 -> x0, local copies, waits for them, and re-layouts: 13.7 us -> none  [the longest x3 5.75 us: phi_column(): augmented = augmented.at[0, width].set(1.0)]
    reduce_sum x6 -> x0, other arithmetic: 12.1 us -> none  [the longest x4 7.07 us: arnoldi(): jnp.sum(current * image)]
    slice x9 -> x0, other arithmetic: 7.07 us -> none  [the longest x2 3.57 us: arnoldi(): buffer[:column + 1]]
  transfers between devices with their start and end apart: 28 -> 0, of which waited for: 19 -> 0; matrix products, arithmetic and copies ran while one was open for 4% -> 0% of each run, Pallas kernels for 0% -> 0%
where the time goes in v1:
time: 49.9 us; the launch traced here: 49.7 us
  Pallas kernels  45.7 us (92%)
  local copies, waits for them, and re-layouts  3.32 us (7%)
  between operations  0.65 us (1%)
    pallas_call x1, Pallas kernels, body(): pl.pallas_call(functools.partial(kernel, n_row, n_col), out_shape=(shape,...  45.7 us
    unnamed x4, local copies, waits for them, and re-layouts  3.32 us

profile of v1, /device:TPU:0, one launch (start us, length us, event | category | flops | bytes accessed | tf_op | source)
XLA Modules:
  0.0 49.7 jit_solution(16084856552262516120)
XLA Ops:
  0.6 45.7 %epirk_section.1 = (f32[512,512]{1,0:T(8,128)}, f32[512,512]{1,0:T(8,128)}) custom-call(f32[512,512]{1,0:T(8,128)} %phase_hbm.1, s32[2,2]{1,0:T(2,128)} %mask_ref.1), custom_call_target="tpu_custom_call" | custom-call | tf_op jit(solution)/shard_map/epirk_section/pallas_call | solution.py:408
  46.3 0.0 copy-start
  46.3 2.4 %copy.6 = f32[512,512]{1,0:T(8,128)} copy(f32[512,512]{1,0:T(8,128)} %get-tuple-element.4) | data formatting | bytes 2097152
  48.7 0.0 copy-done
  48.7 1.0 %copy.7 = f32[512,512]{1,0:T(8,128)} copy(f32[512,512]{1,0:T(8,128)S(1)} %copy-done) | data formatting | bytes 2097152
Async XLA Ops:
  46.3 2.4 %copy-start = (f32[512,512]{1,0:T(8,128)S(1)}, f32[512,512]{1,0:T(8,128)}, u32[]{:S(2)}) copy-start(f32[512,512]{1,0:T(8,128)} %get-tuple-element.5) | copy-start | bytes 3145732

commit v2 on v1

--- a/solution.py
+++ b/solution.py
@@ -10,7 +10,8 @@
 TILE = 256
 HALO = 8
 LANES = 128
-CHUNK = 16
+CHUNK = 64
+FINAL = 64
 MOMENTS = 6
 MESH = pl.DeviceIdType.MESH
 
@@ -110,18 +111,28 @@
     out_strip, in_side, in_corner, row_buf, gather,
     local_sem, side_send, side_recv, red_send, red_recv,
 ):
-    rows, cols = upd.shape
-    width = cols + LANES
+    blocks, rows, _ = upd.shape
+    cols = blocks * LANES
     tall = rows + 2 * HALO
     n_dev = n_row * n_col
     my_row = lax.axis_index("row")
     my_col = lax.axis_index("col")
     me = my_row * n_col + my_col
 
-    load = pltpu.make_async_copy(
-        phase_hbm, ph.at[pl.ds(HALO, rows), pl.ds(0, cols)], local_sem.at[0]
-    )
-    load.start()
+    def load(j):
+        return pltpu.make_async_copy(
+            phase_hbm.at[:, pl.ds(j * LANES, LANES)],
+            ph.at[j, pl.ds(HALO, rows)],
+            local_sem.at[j],
+        )
+
+    def put(j, src, dst, base):
+        return pltpu.make_async_copy(
+            src.at[j], dst.at[:, pl.ds(j * LANES, LANES)], local_sem.at[base + j]
+        )
+
+    for j in range(blocks):
+        load(j).start()
 
     barrier = pltpu.get_barrier_semaphore()
 
@@ -172,18 +183,24 @@
         cut = pl.ds(j * TILE, TILE)
         out_strip[0, HALO:, cut] = jnp.full((HALO, TILE), value[0][j], jnp.float32)
         out_strip[1, HALO:, cut] = jnp.full((HALO, TILE), value[-1][j], jnp.float32)
+    for j in range(blocks):
         for i in range(tile_rows):
-            a2[pl.ds(HALO + i * TILE, TILE), cut] = jnp.full((TILE, TILE), value[i][j], jnp.float32)
+            a2[j, pl.ds(HALO + i * TILE, TILE), :] = jnp.full(
+                (TILE, LANES), value[i][j * LANES // TILE], jnp.float32
+            )
     for i in range(tile_rows):
         cut = pl.ds(i * TILE, TILE)
         out_strip[2, HALO:, cut] = jnp.full((HALO, TILE), value[i][0], jnp.float32)
         out_strip[3, HALO:, cut] = jnp.full((HALO, TILE), value[i][-1], jnp.float32)
 
-    load.wait()
-    out_strip[0, :HALO, :] = ph[pl.ds(HALO, HALO), pl.ds(0, cols)]
-    out_strip[1, :HALO, :] = ph[pl.ds(rows, HALO), pl.ds(0, cols)]
-    out_strip[2, :HALO, :] = ph[pl.ds(HALO, rows), pl.ds(0, LANES)].T[:HALO]
-    out_strip[3, :HALO, :] = ph[pl.ds(HALO, rows), pl.ds(cols - LANES, LANES)].T[LANES - HALO:]
+    for j in range(blocks):
+        load(j).wait()
+    for j in range(blocks):
+        cut = pl.ds(j * LANES, LANES)
+        out_strip[0, :HALO, cut] = ph[j, pl.ds(HALO, HALO), :]
+        out_strip[1, :HALO, cut] = ph[j, pl.ds(rows, HALO), :]
+    out_strip[2, :HALO, :] = ph[0, pl.ds(HALO, rows), :].T[:HALO]
+    out_strip[3, :HALO, :] = ph[blocks - 1, pl.ds(HALO, rows), :].T[LANES - HALO:]
 
     pl.semaphore_wait(barrier, n_dev - 1)
 
@@ -219,74 +236,73 @@
             side_arrival(k).wait_recv()
 
     lane = lax.broadcasted_iota(jnp.int32, (HALO, LANES), 1)
-    halo_lanes = pl.ds(cols, LANES)
     gap = jnp.zeros((LANES - 2 * HALO, rows), jnp.float32)
     for part, ref in ((slice(0, HALO), ph), (slice(HALO, 2 * HALO), a2)):
-        ref[pl.ds(0, HALO), pl.ds(0, cols)] = in_side[0, part, :]
-        ref[pl.ds(HALO + rows, HALO), pl.ds(0, cols)] = in_side[1, part, :]
-        ref[pl.ds(HALO, rows), halo_lanes] = jnp.concatenate(
+        for j in range(blocks):
+            cut = pl.ds(j * LANES, LANES)
+            ref[j, pl.ds(0, HALO), :] = in_side[0, part, cut]
+            ref[j, pl.ds(HALO + rows, HALO), :] = in_side[1, part, cut]
+        ref[blocks, pl.ds(HALO, rows), :] = jnp.concatenate(
             [in_side[3, part, :], gap, in_side[2, part, :]], axis=0
         ).T
-        ref[pl.ds(0, HALO), halo_lanes] = jnp.where(
+        ref[blocks, pl.ds(0, HALO), :] = jnp.where(
             lane < LANES // 2, in_corner[1, part, :], in_corner[0, part, :]
         )
-        ref[pl.ds(HALO + rows, HALO), halo_lanes] = jnp.where(
+        ref[blocks, pl.ds(HALO + rows, HALO), :] = jnp.where(
             lane < LANES // 2, in_corner[3, part, :], in_corner[2, part, :]
         )
 
-    def around(x, low, count):
-        high = x.shape[0]
-        centre = x[low:low + count]
-        total = (
-            pltpu.roll(x, 1, 0)[low:low + count]
-            + pltpu.roll(x, high - 1, 0)[low:low + count]
-            + pltpu.roll(centre, 1, 1)
-            + pltpu.roll(centre, width - 1, 1)
-        )
-        return centre, total
-
-    def fold(x):
-        total = None
-        for i in range(0, x.shape[0], 8):
-            for j in range(0, cols, LANES):
-                piece = x[i:i + 8, j:j + LANES]
-                total = piece if total is None else total + piece
-        return total
+    def around(field, at, above, below, count, outer):
+        column = lax.broadcasted_iota(jnp.int32, (count, LANES), 1)
+        centre = [field[j, at, :] for j in range(blocks + 1)]
+        ahead = [pltpu.roll(x, 1, 1) for x in centre]
+        behind = [pltpu.roll(x, LANES - 1, 1) for x in centre]
+        n = blocks + 1
+        for j in range(n if outer else blocks):
+            near = (
+                field[j, above, :]
+                + field[j, below, :]
+                + jnp.where(column == 0, ahead[(j - 1) % n], ahead[j])
+                + jnp.where(column == LANES - 1, behind[(j + 1) % n], behind[j])
+            )
+            yield j, centre[j], near
 
     def sweep(field, finish, n_sums, halo):
         if halo:
-            finish(*around(field[pl.ds(0, 2 * HALO), :], 0, HALO), pl.ds(0, HALO))
-            finish(
-                *around(field[pl.ds(tall - 2 * HALO, 2 * HALO), :], HALO, HALO),
-                pl.ds(tall - HALO, HALO),
-            )
+            for first in (1, tall - 1 - HALO):
+                at, above, below = (pl.ds(first + shift, HALO) for shift in (0, -1, 1))
+                for j, centre, near in around(field, at, above, below, HALO, True):
+                    finish(j, centre, near, at)
 
         def step(i, sums):
             start = pl.multiple_of(i * CHUNK, 8)
-            x = field[pl.ds(start, CHUNK + 2 * HALO), :]
-            terms = finish(
-                *around(x, HALO, CHUNK), pl.ds(pl.multiple_of(start + HALO, 8), CHUNK)
-            )
-            return tuple(s + fold(t) for s, t in zip(sums, terms))
-
-        zero = jnp.zeros((8, LANES), jnp.float32)
+            at = pl.ds(pl.multiple_of(start + HALO, 8), CHUNK)
+            above = pl.ds(start + (HALO - 1), CHUNK)
+            below = pl.ds(start + (HALO + 1), CHUNK)
+            for j, centre, near in around(field, at, above, below, CHUNK, halo):
+                terms = finish(j, centre, near, at)
+                if j < blocks:
+                    sums = tuple(s + t for s, t in zip(sums, terms))
+            return sums
+
+        zero = jnp.zeros((CHUNK, LANES), jnp.float32)
         return lax.fori_loop(0, rows // CHUNK, step, (zero,) * n_sums)
 
-    def force_of(centre, near, at):
-        act2 = a2[at, :]
+    def force_of(j, centre, near, at):
+        act2 = a2[j, at, :]
         square = centre * centre
         act = act2 * (1.0 / diffusion)
-        q[at, :] = act * (1.0 - 3.0 * square)
-        u0[at, :] = act2 * (near - 4.0 * centre) + act * ((1.0 - square) * centre)
+        q[j, at, :] = act * (1.0 - 3.0 * square)
+        u0[j, at, :] = act2 * (near - 4.0 * centre) + act * ((1.0 - square) * centre)
         return ()
 
     sweep(ph, force_of, 0, True)
 
     def power(dst, with_start):
-        def finish(centre, near, at):
-            image = a2[at, :] * near + q[at, :] * centre
+        def finish(j, centre, near, at):
+            image = a2[j, at, :] * near + q[j, at, :] * centre
             if dst is not None:
-                dst[at, :] = image
+                dst[j, at, :] = image
             cross = centre * image
             if dst is None:
                 return (cross,)
@@ -340,9 +356,6 @@
             for k in range(MOMENTS)
         ]
 
-    def spread(x, count, wide):
-        return jnp.broadcast_to(x, (count, wide))
-
     diag, lower, coefs = lanczos(moments(u0, u1, u2, 0))
     sub = lax.broadcasted_iota(jnp.int32, (8, LANES), 0)
     scale = jnp.where(sub < 4, 0.5, 1.0).astype(jnp.float32)
@@ -351,13 +364,14 @@
     full = [m[4:5, 0:1] for m in mixed]
 
     def section_of(at, out_at):
-        x0, x1, x2 = u0[at, :], u1[at, :], u2[at, :]
-        here = ph[at, :]
-        shift = half[0] * x0 + half[1] * x1 + half[2] * x2
-        w0[at, :] = (a2[at, :] * (-1.0 / diffusion)) * shift * shift * (shift + 3.0 * here)
-        if out_at is not None:
-            sec[out_at, :] = (here + shift)[:, :cols]
-            upd[out_at, :] = (here + full[0] * x0 + full[1] * x1 + full[2] * x2)[:, :cols]
+        for j in range(blocks + 1):
+            x0, x1, x2 = u0[j, at, :], u1[j, at, :], u2[j, at, :]
+            here = ph[j, at, :]
+            shift = half[0] * x0 + half[1] * x1 + half[2] * x2
+            w0[j, at, :] = (a2[j, at, :] * (-1.0 / diffusion)) * shift * shift * (shift + 3.0 * here)
+            if out_at is not None and j < blocks:
+                sec[j, out_at, :] = here + shift
+                upd[j, out_at, :] = here + full[0] * x0 + full[1] * x1 + full[2] * x2
 
     section_of(pl.ds(0, HALO), None)
     section_of(pl.ds(tall - HALO, HALO), None)
@@ -368,8 +382,8 @@
         return carry
 
     lax.fori_loop(0, rows // CHUNK, section_step, 0)
-    put_sec = pltpu.make_async_copy(sec, sec_hbm, local_sem.at[1])
-    put_sec.start()
+    for j in range(blocks):
+        put(j, sec, sec_hbm, blocks).start()
 
     diag, lower, coefs = lanczos(moments(w0, w1, w2, 1))
     third = [
@@ -377,32 +391,33 @@
         for m in to_powers(phi_weights(diag, lower, jnp.ones((8, LANES), jnp.float32), 3), coefs)
     ]
 
-    def final_step(i, carry):
-        start = pl.multiple_of(i * CHUNK, 8)
-        at = pl.ds(pl.multiple_of(start + HALO, 8), CHUNK)
-        cut = pl.ds(0, cols)
-        out_at = pl.ds(start, CHUNK)
-        upd[out_at, :] = upd[out_at, :] + (
-            third[0] * w0[at, cut] + third[1] * w1[at, cut] + third[2] * w2[at, cut]
-        )
-        return carry
-
-    lax.fori_loop(0, rows // CHUNK, final_step, 0)
-    put_upd = pltpu.make_async_copy(upd, upd_hbm, local_sem.at[2])
-    put_upd.start()
+    for j in range(blocks):
+        def final_step(i, carry, j=j):
+            start = pl.multiple_of(i * FINAL, 8)
+            at = pl.ds(pl.multiple_of(start + HALO, 8), FINAL)
+            out_at = pl.ds(start, FINAL)
+            upd[j, out_at, :] = upd[j, out_at, :] + (
+                third[0] * w0[j, at, :] + third[1] * w1[j, at, :] + third[2] * w2[j, at, :]
+            )
+            return carry
+
+        lax.fori_loop(0, rows // FINAL, final_step, 0)
+        put(j, upd, upd_hbm, 2 * blocks).start()
     for k in range(8):
         @pl.when(exists(k))
         def _(k=k):
             side_copy(k).wait_send()
-    put_sec.wait()
-    put_upd.wait()
+    for j in range(blocks):
+        put(j, sec, sec_hbm, blocks).wait()
+        put(j, upd, upd_hbm, 2 * blocks).wait()
 
 
 def body(n_row, n_col, phase, tile_mask):
     rows, cols = phase.shape
     n_dev = n_row * n_col
-    block = pltpu.VMEM((rows + 2 * HALO, cols + LANES), jnp.float32)
-    flat = pltpu.VMEM((rows, cols), jnp.float32)
+    blocks = cols // LANES
+    block = pltpu.VMEM((blocks + 1, rows + 2 * HALO, LANES), jnp.float32)
+    flat = pltpu.VMEM((blocks, rows, LANES), jnp.float32)
     shape = jax.ShapeDtypeStruct((rows, cols), jnp.float32)
     hbm = pl.BlockSpec(memory_space=pl.ANY)
     return pl.pallas_call(
@@ -416,7 +431,7 @@
             pltpu.VMEM((4, 2 * HALO, LANES), jnp.float32),
             pltpu.VMEM((2, 1, LANES), jnp.float32),
             pltpu.VMEM((2, n_dev, 1, LANES), jnp.float32),
-            pltpu.SemaphoreType.DMA((3,)),
+            pltpu.SemaphoreType.DMA((3 * blocks,)),
             pltpu.SemaphoreType.DMA((8,)),
             pltpu.SemaphoreType.DMA((8,)),
             pltpu.SemaphoreType.DMA((2,)),

time: 49.9 us -> 38.3 us (0.77)
  Pallas kernels: 45.7 us -> 34.1 us
    pallas_call x1, Pallas kernels: 45.7 us -> 34.1 us  [body(): pl.pallas_call(functools.partial(kernel, n_row, n_col), out_shape=(shape,...]
where the time goes in v2:
time: 38.3 us; the launch traced here: 38.1 us
  Pallas kernels  34.1 us (89%)
  local copies, waits for them, and re-layouts  3.32 us (9%)
  between operations  0.65 us (2%)
    pallas_call x1, Pallas kernels, body(): pl.pallas_call(functools.partial(kernel, n_row, n_col), out_shape=(shape,...  34.1 us
    unnamed x4, local copies, waits for them, and re-layouts  3.32 us

profile of v2, /device:TPU:0, one launch (start us, length us, event | category | flops | bytes accessed | tf_op | source)
XLA Modules:
  0.0 38.1 jit_solution(14322096581993456483)
XLA Ops:
  0.6 34.1 %epirk_section.1 = (f32[512,512]{1,0:T(8,128)}, f32[512,512]{1,0:T(8,128)}) custom-call(f32[512,512]{1,0:T(8,128)} %phase_hbm.1, s32[2,2]{1,0:T(2,128)} %mask_ref.1), custom_call_target="tpu_custom_call" | custom-call | tf_op jit(solution)/shard_map/epirk_section/pallas_call | solution.py:423
  34.7 0.0 copy-start
  34.8 2.4 %copy.6 = f32[512,512]{1,0:T(8,128)} copy(f32[512,512]{1,0:T(8,128)} %get-tuple-element.4) | data formatting | bytes 2097152
  37.1 0.0 copy-done
  37.1 1.0 %copy.7 = f32[512,512]{1,0:T(8,128)} copy(f32[512,512]{1,0:T(8,128)S(1)} %copy-done) | data formatting | bytes 2097152
Async XLA Ops:
  34.7 2.4 %copy-start = (f32[512,512]{1,0:T(8,128)S(1)}, f32[512,512]{1,0:T(8,128)}, u32[]{:S(2)}) copy-start(f32[512,512]{1,0:T(8,128)} %get-tuple-element.5) | copy-start | bytes 3145732

commit v3 on v2

--- a/solution.py
+++ b/solution.py
@@ -10,7 +10,7 @@
 TILE = 256
 HALO = 8
 LANES = 128
-CHUNK = 64
+CHUNK = 128
 FINAL = 64
 MOMENTS = 6
 MESH = pl.DeviceIdType.MESH
@@ -106,13 +106,13 @@
 
 
 def kernel(
-    n_row, n_col, phase_hbm, mask_ref, upd_hbm, sec_hbm,
-    ph, a2, q, u0, u1, u2, w0, w1, w2, upd, sec,
+    n_row, n_col, phase_hbm, mask_hbm, upd, sec,
+    ph, a2, q, u0, u1, u2, w0, w1, w2, mask_ref,
     out_strip, in_side, in_corner, row_buf, gather,
     local_sem, side_send, side_recv, red_send, red_recv,
 ):
-    blocks, rows, _ = upd.shape
-    cols = blocks * LANES
+    rows, cols = upd.shape
+    blocks = cols // LANES
     tall = rows + 2 * HALO
     n_dev = n_row * n_col
     my_row = lax.axis_index("row")
@@ -126,13 +126,10 @@
             local_sem.at[j],
         )
 
-    def put(j, src, dst, base):
-        return pltpu.make_async_copy(
-            src.at[j], dst.at[:, pl.ds(j * LANES, LANES)], local_sem.at[base + j]
-        )
-
     for j in range(blocks):
         load(j).start()
+    load_mask = pltpu.make_async_copy(mask_hbm, mask_ref, local_sem.at[blocks])
+    load_mask.start()
 
     barrier = pltpu.get_barrier_semaphore()
 
@@ -140,11 +137,21 @@
         peer = lax.rem(me + d, n_dev)
         return {"row": peer // n_col, "col": lax.rem(peer, n_col)}
 
-    def greet(d, carry):
-        pl.semaphore_signal(barrier, inc=1, device_id=peer_of(d), device_id_type=MESH)
-        return carry
-
-    lax.fori_loop(1, n_dev, greet, 0)
+    def far_first(act):
+        for k in range(n_col):
+            col = jnp.where(2 * my_col >= n_col, k, n_col - 1 - k)
+            away = (col != my_col).astype(jnp.int32)
+
+            def one(r, carry, col=col):
+                act({"row": lax.rem(my_row + r, n_row), "col": col})
+                return carry
+
+            lax.fori_loop(1 - away, n_row, one, 0)
+
+    def greet(peer):
+        pl.semaphore_signal(barrier, inc=1, device_id=peer, device_id_type=MESH)
+
+    far_first(greet)
 
     def exists(k):
         dr, dc = STEPS[k]
@@ -174,6 +181,7 @@
             else:
                 in_corner[k - 4] = jnp.zeros((2 * HALO, LANES), jnp.float32)
 
+    load_mask.wait()
     tile_rows, tile_cols = rows // TILE, cols // TILE
     value = [
         [mask_ref[i, j].astype(jnp.float32) * diffusion for j in range(tile_cols)]
@@ -323,18 +331,17 @@
         row_buf[index] = row
         gather[index, me] = row
 
-        def send(d, carry):
+        def send(peer):
             pltpu.make_async_remote_copy(
                 src_ref=row_buf.at[index],
                 dst_ref=gather.at[index, me],
                 send_sem=red_send.at[index],
                 recv_sem=red_recv.at[index],
-                device_id=peer_of(d),
+                device_id=peer,
                 device_id_type=MESH,
             ).start()
-            return carry
-
-        lax.fori_loop(1, n_dev, send, 0)
+
+        far_first(send)
         others = gather.at[index, pl.ds(0, n_dev - 1)]
         done = pltpu.make_async_remote_copy(
             src_ref=others,
@@ -345,7 +352,6 @@
             device_id_type=MESH,
         )
         done.wait_recv()
-        done.wait_send()
         total = jnp.sum(gather[index], axis=0)
         total = jnp.broadcast_to(total, (8, LANES))
         spot = lax.broadcasted_iota(jnp.int32, (8, LANES), 1)
@@ -370,8 +376,8 @@
             shift = half[0] * x0 + half[1] * x1 + half[2] * x2
             w0[j, at, :] = (a2[j, at, :] * (-1.0 / diffusion)) * shift * shift * (shift + 3.0 * here)
             if out_at is not None and j < blocks:
-                sec[j, out_at, :] = here + shift
-                upd[j, out_at, :] = here + full[0] * x0 + full[1] * x1 + full[2] * x2
+                sec[out_at, pl.ds(j * LANES, LANES)] = here + shift
+                upd[out_at, pl.ds(j * LANES, LANES)] = here + full[0] * x0 + full[1] * x1 + full[2] * x2
 
     section_of(pl.ds(0, HALO), None)
     section_of(pl.ds(tall - HALO, HALO), None)
@@ -382,8 +388,6 @@
         return carry
 
     lax.fori_loop(0, rows // CHUNK, section_step, 0)
-    for j in range(blocks):
-        put(j, sec, sec_hbm, blocks).start()
 
     diag, lower, coefs = lanczos(moments(w0, w1, w2, 1))
     third = [
@@ -396,20 +400,23 @@
             start = pl.multiple_of(i * FINAL, 8)
             at = pl.ds(pl.multiple_of(start + HALO, 8), FINAL)
             out_at = pl.ds(start, FINAL)
-            upd[j, out_at, :] = upd[j, out_at, :] + (
+            cut = pl.ds(j * LANES, LANES)
+            upd[out_at, cut] = upd[out_at, cut] + (
                 third[0] * w0[j, at, :] + third[1] * w1[j, at, :] + third[2] * w2[j, at, :]
             )
             return carry
 
         lax.fori_loop(0, rows // FINAL, final_step, 0)
-        put(j, upd, upd_hbm, 2 * blocks).start()
+    for index in range(2):
+        others = gather.at[index, pl.ds(0, n_dev - 1)]
+        pltpu.make_async_remote_copy(
+            src_ref=others, dst_ref=others, send_sem=red_send.at[index], recv_sem=red_recv.at[index],
+            device_id=peer_of(1), device_id_type=MESH,
+        ).wait_send()
     for k in range(8):
         @pl.when(exists(k))
         def _(k=k):
             side_copy(k).wait_send()
-    for j in range(blocks):
-        put(j, sec, sec_hbm, blocks).wait()
-        put(j, upd, upd_hbm, 2 * blocks).wait()
 
 
 def body(n_row, n_col, phase, tile_mask):
@@ -417,29 +424,34 @@
     n_dev = n_row * n_col
     blocks = cols // LANES
     block = pltpu.VMEM((blocks + 1, rows + 2 * HALO, LANES), jnp.float32)
-    flat = pltpu.VMEM((blocks, rows, LANES), jnp.float32)
     shape = jax.ShapeDtypeStruct((rows, cols), jnp.float32)
-    hbm = pl.BlockSpec(memory_space=pl.ANY)
+    vmem = pl.BlockSpec(memory_space=pltpu.VMEM)
     return pl.pallas_call(
         functools.partial(kernel, n_row, n_col),
         out_shape=(shape, shape),
-        in_specs=[hbm, pl.BlockSpec(memory_space=pltpu.SMEM)],
-        out_specs=(hbm, hbm),
-        scratch_shapes=[block] * 9 + [flat] * 2 + [
+        in_specs=[pl.BlockSpec(memory_space=pltpu.HBM), pl.BlockSpec(memory_space=pltpu.HBM)],
+        out_specs=(vmem, vmem),
+        scratch_shapes=[block] * 9 + [
+            pltpu.SMEM(tile_mask.shape, jnp.int32),
             pltpu.VMEM((4, 2 * HALO, cols), jnp.float32),
             pltpu.VMEM((4, 2 * HALO, cols), jnp.float32),
             pltpu.VMEM((4, 2 * HALO, LANES), jnp.float32),
             pltpu.VMEM((2, 1, LANES), jnp.float32),
             pltpu.VMEM((2, n_dev, 1, LANES), jnp.float32),
-            pltpu.SemaphoreType.DMA((3 * blocks,)),
+            pltpu.SemaphoreType.DMA((blocks + 1,)),
             pltpu.SemaphoreType.DMA((8,)),
             pltpu.SemaphoreType.DMA((8,)),
             pltpu.SemaphoreType.DMA((2,)),
             pltpu.SemaphoreType.DMA((2,)),
         ],
-        compiler_params=pltpu.CompilerParams(collective_id=0, has_side_effects=True),
+        compiler_params=pltpu.CompilerParams(
+            collective_id=0, has_side_effects=True, vmem_limit_bytes=24 << 20
+        ),
         name="epirk_section",
-    )(phase, tile_mask)
+    )(
+        pltpu.with_memory_space_constraint(phase, pltpu.HBM),
+        pltpu.with_memory_space_constraint(tile_mask, pltpu.HBM),
+    )
 
 
 def solution(mesh):

time: 38.3 us -> 33.5 us (0.87)
  Pallas kernels: 34.1 us -> 30.8 us
  local copies, waits for them, and re-layouts: 3.32 us -> 1.94 us
    pallas_call x1, Pallas kernels: 34.1 us -> 30.8 us  [body(): pl.pallas_call(functools.partial(kernel, n_row, n_col), out_shape=(shape,...]
    unnamed x4 -> x2, local copies, waits for them, and re-layouts: 3.32 us -> 1.94 us
where the time goes in v3:
time: 33.5 us; the launch traced here: 33.4 us
  Pallas kernels  30.8 us (92%)
  local copies, waits for them, and re-layouts  1.94 us (6%)
  between operations  0.64 us (2%)
    pallas_call x1, Pallas kernels, body(): pl.pallas_call(functools.partial(kernel, n_row, n_col), out_shape=(shape,...  30.8 us
    unnamed x2, local copies, waits for them, and re-layouts  1.94 us

profile of v3, /device:TPU:0, one launch (start us, length us, event | category | flops | bytes accessed | tf_op | source)
XLA Modules:
  0.0 33.4 jit_solution(8517893602622989871)
XLA Ops:
  0.6 30.8 %epirk_section.1 = (f32[512,512]{1,0:T(8,128)S(1)}, f32[512,512]{1,0:T(8,128)S(1)}) custom-call(f32[512,512]{1,0:T(8,128)} %phase_hbm.1, s32[2,2]{1,0:T(2,128)} %mask_hbm.1), custom_call_target="tpu_custom_call" | custom-call | tf_op jit(solution)/shard_map/epirk_section/pallas_call | solution.py:429
  31.4 1.0 %copy.6 = f32[512,512]{1,0:T(8,128)} copy(f32[512,512]{1,0:T(8,128)S(1)} %get-tuple-element.4) | data formatting | bytes 2097152
  32.4 1.0 %copy.7 = f32[512,512]{1,0:T(8,128)} copy(f32[512,512]{1,0:T(8,128)S(1)} %get-tuple-element.5) | data formatting | bytes 2097152

commit v4 on v3

--- a/solution.py
+++ b/solution.py
@@ -12,6 +12,7 @@
 LANES = 128
 CHUNK = 128
 FINAL = 64
+PIECES = 2
 MOMENTS = 6
 MESH = pl.DeviceIdType.MESH
 
@@ -320,7 +321,7 @@
 
         return finish
 
-    def moments(b0, b1, b2, index):
+    def moments(b0, b1, b2, index, meanwhile):
         sums = sweep(b0, power(b1, True), 3, True)
         sums += sweep(b1, power(b2, False), 2, True)
         sums += sweep(b2, power(None, False), 1, False)
@@ -342,6 +343,7 @@
             ).start()
 
         far_first(send)
+        meanwhile()
         others = gather.at[index, pl.ds(0, n_dev - 1)]
         done = pltpu.make_async_remote_copy(
             src_ref=others,
@@ -362,34 +364,48 @@
             for k in range(MOMENTS)
         ]
 
-    diag, lower, coefs = lanczos(moments(u0, u1, u2, 0))
+    diag, lower, coefs = lanczos(moments(u0, u1, u2, 0, lambda: None))
     sub = lax.broadcasted_iota(jnp.int32, (8, LANES), 0)
     scale = jnp.where(sub < 4, 0.5, 1.0).astype(jnp.float32)
     mixed = to_powers(phi_weights(diag, lower, scale, 1), coefs)
     half = [0.5 * m[0:1, 0:1] for m in mixed]
     full = [m[4:5, 0:1] for m in mixed]
 
-    def section_of(at, out_at):
+    def shift_of(j, at):
+        return half[0] * u0[j, at, :] + half[1] * u1[j, at, :] + half[2] * u2[j, at, :]
+
+    def remainder_of(at):
         for j in range(blocks + 1):
-            x0, x1, x2 = u0[j, at, :], u1[j, at, :], u2[j, at, :]
-            here = ph[j, at, :]
-            shift = half[0] * x0 + half[1] * x1 + half[2] * x2
-            w0[j, at, :] = (a2[j, at, :] * (-1.0 / diffusion)) * shift * shift * (shift + 3.0 * here)
-            if out_at is not None and j < blocks:
-                sec[out_at, pl.ds(j * LANES, LANES)] = here + shift
-                upd[out_at, pl.ds(j * LANES, LANES)] = here + full[0] * x0 + full[1] * x1 + full[2] * x2
-
-    section_of(pl.ds(0, HALO), None)
-    section_of(pl.ds(tall - HALO, HALO), None)
-
-    def section_step(i, carry):
-        start = pl.multiple_of(i * CHUNK, 8)
-        section_of(pl.ds(pl.multiple_of(start + HALO, 8), CHUNK), pl.ds(start, CHUNK))
+            shift = shift_of(j, at)
+            weight = a2[j, at, :] * (-1.0 / diffusion)
+            w0[j, at, :] = weight * shift * shift * (shift + 3.0 * ph[j, at, :])
+
+    remainder_of(pl.ds(0, HALO))
+    remainder_of(pl.ds(tall - HALO, HALO))
+
+    def remainder_step(i, carry):
+        remainder_of(pl.ds(pl.multiple_of(i * FINAL + HALO, 8), FINAL))
         return carry
 
-    lax.fori_loop(0, rows // CHUNK, section_step, 0)
-
-    diag, lower, coefs = lanczos(moments(w0, w1, w2, 1))
+    lax.fori_loop(0, rows // FINAL, remainder_step, 0)
+
+    def results():
+        def result_step(i, carry):
+            start = pl.multiple_of(i * FINAL, 8)
+            at = pl.ds(pl.multiple_of(start + HALO, 8), FINAL)
+            out_at = pl.ds(start, FINAL)
+            for j in range(blocks):
+                cut = pl.ds(j * LANES, LANES)
+                here = ph[j, at, :]
+                sec[out_at, cut] = here + shift_of(j, at)
+                upd[out_at, cut] = here + (
+                    full[0] * u0[j, at, :] + full[1] * u1[j, at, :] + full[2] * u2[j, at, :]
+                )
+            return carry
+
+        lax.fori_loop(0, rows // FINAL, result_step, 0)
+
+    diag, lower, coefs = lanczos(moments(w0, w1, w2, 1, results))
     third = [
         remainder_weight * m[0:1, 0:1]
         for m in to_powers(phi_weights(diag, lower, jnp.ones((8, LANES), jnp.float32), 3), coefs)
@@ -419,6 +435,21 @@
             side_copy(k).wait_send()
 
 
+def flush(upd, sec, upd_hbm, sec_hbm, sems):
+    step = upd.shape[0] // PIECES
+    copies = [
+        pltpu.make_async_copy(
+            src.at[pl.ds(i * step, step)], dst.at[pl.ds(i * step, step)], sems.at[k, i]
+        )
+        for i in range(PIECES)
+        for k, (src, dst) in enumerate(((upd, upd_hbm), (sec, sec_hbm)))
+    ]
+    for copy in copies:
+        copy.start()
+    for copy in copies:
+        copy.wait()
+
+
 def body(n_row, n_col, phase, tile_mask):
     rows, cols = phase.shape
     n_dev = n_row * n_col
@@ -426,7 +457,7 @@
     block = pltpu.VMEM((blocks + 1, rows + 2 * HALO, LANES), jnp.float32)
     shape = jax.ShapeDtypeStruct((rows, cols), jnp.float32)
     vmem = pl.BlockSpec(memory_space=pltpu.VMEM)
-    return pl.pallas_call(
+    updated, section = pl.pallas_call(
         functools.partial(kernel, n_row, n_col),
         out_shape=(shape, shape),
         in_specs=[pl.BlockSpec(memory_space=pltpu.HBM), pl.BlockSpec(memory_space=pltpu.HBM)],
@@ -452,6 +483,16 @@
         pltpu.with_memory_space_constraint(phase, pltpu.HBM),
         pltpu.with_memory_space_constraint(tile_mask, pltpu.HBM),
     )
+    hbm = pl.BlockSpec(memory_space=pltpu.HBM)
+    return pl.pallas_call(
+        flush,
+        out_shape=(shape, shape),
+        in_specs=(vmem, vmem),
+        out_specs=(hbm, hbm),
+        scratch_shapes=[pltpu.SemaphoreType.DMA((2, PIECES))],
+        compiler_params=pltpu.CompilerParams(vmem_limit_bytes=8 << 20),
+        name="flush",
+    )(updated, section)
 
 
 def solution(mesh):

time: 33.5 us -> 32.6 us (0.973)
  local copies, waits for them, and re-layouts: 1.94 us -> 0 us
  Pallas kernels: 30.8 us -> 31.8 us
    unnamed x2 -> x0, local copies, waits for them, and re-layouts: 1.94 us -> none
    pallas_call x0 -> x1, Pallas kernels: none -> 1.35 us  [body(): pl.pallas_call(flush, out_shape=(shape, shape), in_specs=(vmem, vmem), ou...]
    pallas_call x1, Pallas kernels: 30.8 us -> 30.4 us  [body(): pl.pallas_call(functools.partial(kernel, n_row, n_col), out_shape=(shape,...]
where the time goes in v4:
time: 32.6 us; the launch traced here: 32.4 us
  Pallas kernels  31.8 us (98%)
  between operations  0.64 us (2%)
    pallas_call x1, Pallas kernels, body(): pl.pallas_call(functools.partial(kernel, n_row, n_col), out_shape=(shape,...  30.4 us
    pallas_call x1, Pallas kernels, body(): pl.pallas_call(flush, out_shape=(shape, shape), in_specs=(vmem, vmem), ou...  1.35 us

profile of v4, /device:TPU:0, one launch (start us, length us, event | category | flops | bytes accessed | tf_op | source)
XLA Modules:
  0.0 32.4 jit_solution(17079124505323873881)
XLA Ops:
  0.6 30.4 %epirk_section.1 = (f32[512,512]{1,0:T(8,128)S(1)}, f32[512,512]{1,0:T(8,128)S(1)}) custom-call(f32[512,512]{1,0:T(8,128)} %phase_hbm.1, s32[2,2]{1,0:T(2,128)} %mask_hbm.1), custom_call_target="tpu_custom_call" | custom-call | tf_op jit(solution)/shard_map/epirk_section/pallas_call | solution.py:460
  31.1 1.3 %flush.1 = (f32[512,512]{1,0:T(8,128)}, f32[512,512]{1,0:T(8,128)}) custom-call(f32[512,512]{1,0:T(8,128)S(1)} %get-tuple-element.4.upd, f32[512,512]{1,0:T(8,128)S(1)} %get-tuple-element.5.sec), custom_call_target="tpu_custom_call" | custom-call | tf_op jit(solution)/shard_map/flush/pallas_call | solution.py:487

commit v5 on v4

--- a/solution.py
+++ b/solution.py
@@ -12,7 +12,7 @@
 LANES = 128
 CHUNK = 128
 FINAL = 64
-PIECES = 2
+PIECES = 4
 MOMENTS = 6
 MESH = pl.DeviceIdType.MESH
 
@@ -107,8 +107,8 @@
 
 
 def kernel(
-    n_row, n_col, phase_hbm, mask_hbm, upd, sec,
-    ph, a2, q, u0, u1, u2, w0, w1, w2, mask_ref,
+    n_row, n_col, phase_hbm, mask_hbm, upd, sec, w0, w1, w2, third,
+    ph, a2, q, u0, u1, u2, mask_ref,
     out_strip, in_side, in_corner, row_buf, gather,
     local_sem, side_send, side_recv, red_send, red_recv,
 ):
@@ -406,23 +406,9 @@
         lax.fori_loop(0, rows // FINAL, result_step, 0)
 
     diag, lower, coefs = lanczos(moments(w0, w1, w2, 1, results))
-    third = [
-        remainder_weight * m[0:1, 0:1]
-        for m in to_powers(phi_weights(diag, lower, jnp.ones((8, LANES), jnp.float32), 3), coefs)
-    ]
-
-    for j in range(blocks):
-        def final_step(i, carry, j=j):
-            start = pl.multiple_of(i * FINAL, 8)
-            at = pl.ds(pl.multiple_of(start + HALO, 8), FINAL)
-            out_at = pl.ds(start, FINAL)
-            cut = pl.ds(j * LANES, LANES)
-            upd[out_at, cut] = upd[out_at, cut] + (
-                third[0] * w0[j, at, :] + third[1] * w1[j, at, :] + third[2] * w2[j, at, :]
-            )
-            return carry
-
-        lax.fori_loop(0, rows // FINAL, final_step, 0)
+    weights = phi_weights(diag, lower, jnp.ones((8, LANES), jnp.float32), 3)
+    for k, m in enumerate(to_powers(weights, coefs)):
+        third[k] = remainder_weight * m
     for index in range(2):
         others = gather.at[index, pl.ds(0, n_dev - 1)]
         pltpu.make_async_remote_copy(
@@ -435,19 +421,37 @@
             side_copy(k).wait_send()
 
 
-def flush(upd, sec, upd_hbm, sec_hbm, sems):
-    step = upd.shape[0] // PIECES
-    copies = [
-        pltpu.make_async_copy(
-            src.at[pl.ds(i * step, step)], dst.at[pl.ds(i * step, step)], sems.at[k, i]
-        )
-        for i in range(PIECES)
-        for k, (src, dst) in enumerate(((upd, upd_hbm), (sec, sec_hbm)))
-    ]
-    for copy in copies:
-        copy.start()
-    for copy in copies:
-        copy.wait()
+def flush(upd, sec, w0, w1, w2, third, upd_hbm, sec_hbm, total, sems):
+    rows, cols = upd.shape
+    step = rows // PIECES
+
+    def copy(k, i):
+        src, dst = ((total, upd_hbm), (sec, sec_hbm))[k]
+        at = pl.ds(i * step, step)
+        return pltpu.make_async_copy(src.at[at], dst.at[at], sems.at[k, i])
+
+    for i in range(PIECES):
+        copy(1, i).start()
+    weight = [third[k, 0:1, :] for k in range(3)]
+    for i in range(PIECES):
+        def part(p, carry, i=i):
+            start = pl.multiple_of(i * step + p * FINAL, 8)
+            at = pl.ds(start, FINAL)
+            inner = pl.ds(pl.multiple_of(start + HALO, 8), FINAL)
+            for j in range(cols // LANES):
+                cut = pl.ds(j * LANES, LANES)
+                total[at, cut] = upd[at, cut] + (
+                    weight[0] * w0[j, inner, :]
+                    + weight[1] * w1[j, inner, :]
+                    + weight[2] * w2[j, inner, :]
+                )
+            return carry
+
+        lax.fori_loop(0, step // FINAL, part, 0)
+        copy(0, i).start()
+    for k in range(2):
+        for i in range(PIECES):
+            copy(k, i).wait()
 
 
 def body(n_row, n_col, phase, tile_mask):
@@ -457,12 +461,14 @@
     block = pltpu.VMEM((blocks + 1, rows + 2 * HALO, LANES), jnp.float32)
     shape = jax.ShapeDtypeStruct((rows, cols), jnp.float32)
     vmem = pl.BlockSpec(memory_space=pltpu.VMEM)
-    updated, section = pl.pallas_call(
+    field = jax.ShapeDtypeStruct((blocks + 1, rows + 2 * HALO, LANES), jnp.float32)
+    small = jax.ShapeDtypeStruct((3, 8, LANES), jnp.float32)
+    parts = pl.pallas_call(
         functools.partial(kernel, n_row, n_col),
-        out_shape=(shape, shape),
+        out_shape=(shape, shape, field, field, field, small),
         in_specs=[pl.BlockSpec(memory_space=pltpu.HBM), pl.BlockSpec(memory_space=pltpu.HBM)],
-        out_specs=(vmem, vmem),
-        scratch_shapes=[block] * 9 + [
+        out_specs=(vmem,) * 6,
+        scratch_shapes=[block] * 6 + [
             pltpu.SMEM(tile_mask.shape, jnp.int32),
             pltpu.VMEM((4, 2 * HALO, cols), jnp.float32),
             pltpu.VMEM((4, 2 * HALO, cols), jnp.float32),
@@ -487,12 +493,14 @@
     return pl.pallas_call(
         flush,
         out_shape=(shape, shape),
-        in_specs=(vmem, vmem),
+        in_specs=(vmem,) * 6,
         out_specs=(hbm, hbm),
-        scratch_shapes=[pltpu.SemaphoreType.DMA((2, PIECES))],
-        compiler_params=pltpu.CompilerParams(vmem_limit_bytes=8 << 20),
+        scratch_shapes=[
+            pltpu.VMEM((rows, cols), jnp.float32), pltpu.SemaphoreType.DMA((2, PIECES))
+        ],
+        compiler_params=pltpu.CompilerParams(vmem_limit_bytes=16 << 20),
         name="flush",
-    )(updated, section)
+    )(*parts)
 
 
 def solution(mesh):

time: 32.6 us -> 32.3 us (level)
  no operation moved by 1% of the time
where the time goes in v5:
time: 32.3 us; the launch traced here: 32.2 us
  Pallas kernels  31.5 us (98%)
  between operations  0.64 us (2%)
    pallas_call x1, Pallas kernels, body(): pl.pallas_call(functools.partial(kernel, n_row, n_col), out_shape=(shape,...  30.1 us
    pallas_call x1, Pallas kernels, body(): pl.pallas_call(flush, out_shape=(shape, shape), in_specs=(vmem,) * 6, out...  1.38 us

profile of v5, /device:TPU:0, one launch (start us, length us, event | category | flops | bytes accessed | tf_op | source)
XLA Modules:
  0.0 32.2 jit_solution(17666071897915379654)
XLA Ops:
  0.6 30.1 %epirk_section.1 = (f32[512,512]{1,0:T(8,128)S(1)}, f32[512,512]{1,0:T(8,128)S(1)}, f32[5,528,128]{2,1,0:T(8,128)S(1)}, f32[5,528,128]{2,1,0:T(8,128)S(1)}, f32[...) custom-call(f32[512,512]{1,0:T(8,128)} %phase_hbm.1, s32[2,2]{1,0:T(2,128)} %mask_hbm.1), custom_call_target="tpu_custom_call" | custom-call | tf_op jit(solution)/shard_map/epirk_section/pallas_call | solution.py:466
  30.8 1.4 %flush.1 = (f32[512,512]{1,0:T(8,128)}, f32[512,512]{1,0:T(8,128)}) custom-call(f32[512,512]{1,0:T(8,128)S(1)} %get-tuple-element.8.upd, f32[512,512]{1,0:T(8,128)S(1)} %get-tuple-element.9.sec, f32[5,528,128]{2,1,0:T(8,128)S(1)} %get-tuple-element.10.w0, f32[5,528,128]{2,1,0:T(8,128)S(1)} %get-tuple-element.11.w1, f32[5,528,128]{2,1,0:T(8,128)S(1)} %get-tuple-element.12.w2, ...), custom_call_target="tpu_custom_call" | custom-call | tf_op jit(solution)/shard_map/flush/pallas_call | solution.py:493
